TPU v7x, 32 devices: a whole 2x2x4 slice. The times are simulated.
32 devices in a mesh: row: 4 (over y, core), col: 8 (over z, x).
Axes of the slice: x: 2, y: 2, z: 4, core: 2. Of those that a mesh axis runs over, the one named last changes fastest.
Arguments:
- acts: bfloat16 [192, 2, 28672], P('col', None, 'row'), may hold values from -6 to 6
- grads: bfloat16 [192, 2, 8192], P('row', None, 'col'), may hold values from -0.3984375 to 0.3984375
- basis_in: bfloat16 [28672, 28672], P('row', 'col'), may hold values from -0.03125 to 0.03125
- basis_out: bfloat16 [8192, 8192], P('col', 'row'), may hold values from -0.0625 to 0.0625
- eigen: bfloat16 [28672, 8192], P('col', 'row'), may hold values from 0.5 to 8
- sketch: bfloat16 [72, 8192], P(None, 'col'), may hold values from -0.0625 to 0.0625
Outputs:
- range_basis: float32 [2, 72, 28672], P(None, None, 'row')
- projected: float32 [2, 72, 8192], P(None, None, 'col')
All inputs are finite; a program needn't handle non-finite values.
Results may differ from a plain program's by a relative error of at most 0.018.
Values may be sent and summed in bfloat16 or wider, within the bound.
A program may use at most 192 MiB of HBM per device.

v0:
```python
import jax
import jax.numpy as jnp
from jax import lax
from jax.sharding import PartitionSpec as P


def on_device(acts, grads, basis_in, basis_out, eigen, sketch):
    full_acts = lax.all_gather(acts, "col", axis=0, tiled=True)
    rows = full_acts
    act_shares = lax.psum_scatter(
        jnp.einsum("tqi,ij->tqj", rows, basis_in, preferred_element_type=jnp.float32),
        "row",
        scatter_dimension=0,
        tiled=True,
    ).astype(jnp.bfloat16)
    full_grads = lax.all_gather(grads, "row", axis=0, tiled=True)
    tokens = full_grads.shape[0]
    queries = full_grads.shape[1]
    flat_grads = full_grads.reshape(tokens * queries, full_grads.shape[2])
    joined = jnp.concatenate([flat_grads, sketch], axis=0)
    joined_sum = lax.psum(
        jnp.dot(joined, basis_out, preferred_element_type=jnp.float32), "col"
    ).astype(jnp.bfloat16)
    grad_rot = joined_sum[: tokens * queries].reshape(tokens, queries, basis_out.shape[1])
    sketch_rot = joined_sum[tokens * queries :]
    rows = grad_rot
    core_sum = jnp.einsum(
        "tqj,tqp->qjp",
        lax.all_gather(act_shares, "row", axis=0, tiled=True),
        rows,
        preferred_element_type=jnp.float32,
    )
    scaled = (core_sum / eigen.astype(jnp.float32)).astype(jnp.bfloat16)
    reduced_part = jnp.einsum("qjp,sp->qsj", scaled, sketch_rot, preferred_element_type=jnp.float32)
    reduced = lax.psum(reduced_part, "row").astype(jnp.bfloat16)
    range_part = jnp.einsum("qsj,ij->qsi", reduced, basis_in, preferred_element_type=jnp.float32)
    range_rows = lax.psum(range_part, "col")
    gram_piece = jnp.einsum("qsi,qri->qsr", range_rows, range_rows, precision=lax.Precision.HIGHEST)
    gram = lax.psum(gram_piece, "row")
    factor = jnp.linalg.cholesky(gram)
    basis_rows = lax.linalg.triangular_solve(factor, range_rows, left_side=True, lower=True)
    mapped_part = jnp.einsum(
        "qsi,ij->qsj", basis_rows.astype(jnp.bfloat16), basis_in, preferred_element_type=jnp.float32
    )
    mapped = lax.psum(mapped_part.astype(jnp.bfloat16), "row")
    core_part = jnp.einsum("qsj,qjp->qsp", mapped, scaled, preferred_element_type=jnp.float32)
    core = lax.psum(core_part.astype(jnp.bfloat16), "col")
    projection_part = jnp.einsum("qsp,op->qso", core, basis_out, preferred_element_type=jnp.float32)
    projected = lax.psum(projection_part.astype(jnp.bfloat16), "row").astype(jnp.float32)
    return (basis_rows, projected)


def solution(mesh):
    in_specs = (
        P("col", None, "row"),
        P("row", None, "col"),
        P("row", "col"),
        P("col", "row"),
        P("col", "row"),
        P(None, "col"),
    )
    out_specs = (P(None, None, "row"), P(None, None, "col"))
    return jax.shard_map(
        on_device, mesh=mesh, in_specs=in_specs, out_specs=out_specs, check_vma=False
    )
```

profile of v0, /device:TPU:0, one launch (start us, length us, event | category | flops | bytes accessed | tf_op | source)
XLA Modules:
  0.0 866.9 jit_solution(3863842434083049462)
XLA Ops:
  7.9 94.1 %all-gather.3.cloned.1.call-done = bf16[192,2,7168]{2,1,0:T(2,128)(2,1)} async-done(((bf16[24,2,7168]{2,1,0:T(2,128)(2,1)}), bf16[192,2,7168]{2,1,0:T(2,128)(2,1)}) %all-gather.3.cloned.1.call-update) | async-done | bytes 5505040 | tf_op jit(solution)/shard_map/all_gather | solution.py:8
  102.0 30.9 %fusion.4 = f32[192,2,3584]{2,0,1:T(8,128)} fusion(bf16[7168,3584]{1,0:T(8,128)(2,1)} %param.8, bf16[192,2,7168]{2,1,0:T(2,128)(2,1)} %all-gather.3.cloned.1.call-done), kind=kOutput, calls=%fused_computation.5 | convolution fusion | flops 19730006016 | bytes 62390272 | tf_op jit(solution)/shard_map/tqi,ij->tqj/dot_general | solution.py:11
  133.0 51.3 %reduce-scatter.2.cloned.1.call-done = f32[48,2,3584]{2,0,1:T(8,128)} async-done(((f32[192,2,3584]{2,0,1:T(8,128)}), f32[48,2,3584]{2,0,1:T(8,128)}) %reduce-scatter.2.cloned.1.call-update) | async-done | bytes 1376272 | tf_op jit(solution)/shard_map/reduce_scatter | solution.py:10
  186.7 8.0 all_gather.9
  195.0 6.2 fusion.18
  201.2 150.4 %all-reduce.14 = bf16[456,2048]{1,0:T(8,128)(2,1)S(1)} all-reduce(f32[456,2048]{1,0:T(8,128)} %fusion.18), channel_id=1, replica_groups=mesh['row'=4,'col'=8] {'col'}, use_global_device_ids=true, to_apply=%region_0.0 | all-reduce | flops 933888 | bytes 5603328 | tf_op jit(solution)/shard_map/psum | solution.py:21
  351.8 2.4 reshape.22
  354.1 16.6 %convert_element_type.32 = f32[3584,2048]{1,0:T(8,128)} convert(bf16[3584,2048]{1,0:T(8,128)(2,1)} %param.10) | non-fusion elementwise | flops 7340032 | bytes 44040192 | tf_op jit(solution)/shard_map/convert_element_type | solution.py:33
  370.8 22.4 %divide_convert_fusion = bf16[2,3584,2048]{2,1,0:T(8,128)(2,1)} fusion(f32[3584,2048]{1,0:T(8,128)} %convert_element_type.32, bf16[192,2,3584]{2,0,1:T(8,128)(2,1)} %all-gather.5.cloned.1.call-done, bf16[192,2,2048]{2,1,0:T(2,128)(2,1)S(1)} %copy-done.2), kind=kOutput, calls=%fused_computation | convolution fusion | flops 5666504704 | bytes 63045632 | tf_op jit(solution)/shard_map/tqj,tqp->qjp/dot_general | solution.py:27
  393.2 14.3 %convolution_bitcast_fusion = f32[2,72,3584]{2,1,0:T(8,128)S(1)} fusion(bf16[2,3584,2048]{2,1,0:T(8,128)(2,1)} %divide_convert_fusion, bf16[456,2048]{1,0:T(8,128)(2,1)} %copy-done.1), kind=kOutput, calls=%fused_computation.8 | convolution fusion | flops 2113929216 | bytes 31719424 | tf_op jit(solution)/shard_map/qjp,sp->qsj/dot_general | solution.py:34
  407.5 39.8 %all-reduce.15 = bf16[2,72,3584]{2,1,0:T(8,128)(2,1)S(1)} all-reduce(f32[2,72,3584]{2,1,0:T(8,128)S(1)} %convolution_bitcast_fusion), channel_id=1, replica_groups=mesh['row'=4,'col'=8] {'row'}, use_global_device_ids=true, to_apply=%region_2.0 | all-reduce | flops 516096 | bytes 3096576 | tf_op jit(solution)/shard_map/psum | solution.py:35
  447.3 26.5 %fusion.2 = f32[2,72,7168]{2,1,0:T(8,128)} fusion(bf16[7168,3584]{1,0:T(8,128)(2,1)} %param.8, bf16[2,72,3584]{2,1,0:T(8,128)(2,1)S(1)} %all-reduce.15), kind=kOutput, calls=%fused_computation.3 | convolution fusion | flops 7398752256 | bytes 56541184 | tf_op jit(solution)/shard_map/qsj,ij->qsi/dot_general | solution.py:36
  474.2 153.0 %all-reduce.7.cloned.1.call-done = f32[2,72,7168]{2,1,0:T(8,128)} async-done(((f32[2,72,7168]{2,1,0:T(8,128)}), f32[2,72,7168]{2,1,0:T(8,128)}) %all-reduce.7.cloned.1.call-update) | async-done | bytes 4128784 | tf_op jit(solution)/shard_map/psum | solution.py:37
  627.2 7.4 fusion.26
  634.6 12.0 %psum.52 = f32[2,72,72]{1,2,0:T(8,128)S(1)} all-reduce(f32[2,72,72]{1,2,0:T(8,128)S(1)} %fusion.26), channel_id=1, replica_groups=mesh['row'=4,'col'=8] {'row'}, use_global_device_ids=true, to_apply=%region_4.0 | all-reduce | flops 10368 | bytes 82944 | tf_op jit(solution)/shard_map/psum | solution.py:39
  646.7 13.2 %custom-call.7 = f32[2,72,72]{2,1,0:T(8,128)S(1)} custom-call(f32[2,72,72]{2,1,0:T(8,128)S(1)} %fusion.24), custom_call_target="Cholesky" | custom-call | tf_op jit(solution)/shard_map/jit(cholesky)/cholesky | solution.py:40
  660.2 11.1 %custom-call.8 = f32[2,1,72,72]{2,3,1,0:T(8,128)S(1)} custom-call(f32[2,1,72,72]{3,2,1,0:T(8,128)S(1)} %select_bitcast_fusion), custom_call_target="InvertDiagBlocksLowerTriangular" | custom-call | tf_op jit(solution)/shard_map/triangular_solve | solution.py:41
  671.3 5.3 fusion.22
  678.6 19.0 %fusion.7 = bf16[2,72,3584]{2,1,0:T(8,128)(2,1)} fusion(bf16[7168,3584]{1,0:T(8,128)(2,1)} %param.8, f32[2,72,7168]{2,1,0:T(8,128)S(1)} %fusion.22), kind=kOutput, calls=%fused_computation.9 | convolution fusion | flops 7400300544 | bytes 56541184 | tf_op jit(solution)/shard_map/qsi,ij->qsj/dot_general | solution.py:42
  698.0 34.3 %all-reduce.9.cloned.1.call-done = bf16[2,72,3584]{2,1,0:T(8,128)(2,1)} async-done(((bf16[2,72,3584]{2,1,0:T(8,128)(2,1)}), bf16[2,72,3584]{2,1,0:T(8,128)(2,1)}) %all-reduce.9.cloned.1.call-update) | async-done | bytes 1032208 | tf_op jit(solution)/shard_map/psum | solution.py:45
  732.3 15.7 %convolution_convert_fusion = bf16[2,72,2048]{2,1,0:T(8,128)(2,1)} fusion(bf16[2,72,3584]{2,1,0:T(8,128)(2,1)} %all-reduce.9.cloned.1.call-done, bf16[2,3584,2048]{2,1,0:T(8,128)(2,1)} %divide_convert_fusion), kind=kOutput, calls=%fused_computation.12 | convolution fusion | flops 2114224128 | bytes 30982144 | tf_op jit(solution)/shard_map/qsj,qjp->qsp/dot_general | solution.py:46
  748.0 74.0 %all-reduce.11.cloned.1.call-done = bf16[2,72,2048]{2,1,0:T(8,128)(2,1)} async-done(((bf16[2,72,2048]{2,1,0:T(8,128)(2,1)}), bf16[2,72,2048]{2,1,0:T(8,128)(2,1)}) %all-reduce.11.cloned.1.call-update) | async-done | bytes 589840 | tf_op jit(solution)/shard_map/psum | solution.py:47
  822.0 4.6 fusion.14
  826.7 31.5 %all-reduce.13.cloned.1.call-done = bf16[2,72,1024]{2,1,0:T(8,128)(2,1)} async-done(((bf16[2,72,1024]{2,1,0:T(8,128)(2,1)}), bf16[2,72,1024]{2,1,0:T(8,128)(2,1)}) %all-reduce.13.cloned.1.call-update) | async-done | bytes 294928 | tf_op jit(solution)/shard_map/psum | solution.py:49
  (36 shorter events, 8.4 us)
Async XLA Ops:
  7.2 94.9 %all-gather.3.cloned.1.call-start = ((), (), s32[]{:S(2)}) async-start(), calls=%async_computation.1 | async-start | bytes 6193152 | tf_op jit(solution)/shard_map/all_gather | solution.py:8
  7.9 176.4 %reduce-scatter.2.cloned.1.call-start = ((), (), s32[]{:S(2)}) async-start(), calls=%async_computation.2 | async-start | bytes 6881280 | tf_op jit(solution)/shard_map/reduce_scatter | solution.py:10
  133.0 53.7 %copy-start.3 = (bf16[48,2,1024]{2,1,0:T(2,128)(2,1)S(1)}, bf16[48,2,1024]{2,1,0:T(2,128)(2,1)}, u32[]{:S(2)}) copy-start(bf16[48,2,1024]{2,1,0:T(2,128)(2,1)} %param.7) | copy-start | bytes 589828
  133.0 62.0 %copy-start.4 = (bf16[72,1024]{1,0:T(8,128)(2,1)S(1)}, bf16[72,1024]{1,0:T(8,128)(2,1)}, u32[]{:S(2)}) copy-start(bf16[72,1024]{1,0:T(8,128)(2,1)} %param.11) | copy-start | bytes 442372
  133.0 237.8 %all-gather.5.cloned.1.call-start = ((), (), s32[]{:S(2)}) async-start(), calls=%async_computation.3 | async-start | bytes 3440640 | tf_op jit(solution)/shard_map/all_gather | solution.py:29
  186.6 440.6 %all-reduce.7.cloned.1.call-start = ((), (), s32[]{:S(2)}) async-start(), calls=%async_computation.4 | async-start | bytes 8257536 | tf_op jit(solution)/shard_map/psum | solution.py:37
  351.6 19.2 %copy-start.1 = (bf16[456,2048]{1,0:T(8,128)(2,1)}, bf16[456,2048]{1,0:T(8,128)(2,1)S(1)}, u32[]{:S(2)}) copy-start(bf16[456,2048]{1,0:T(8,128)(2,1)S(1)} %all-reduce.14) | copy-start | bytes 5603332
  354.1 16.6 %copy-start.2 = (bf16[192,2,2048]{2,1,0:T(2,128)(2,1)S(1)}, bf16[192,2,2048]{2,1,0:T(2,128)(2,1)}, u32[]{:S(2)}) copy-start(bf16[192,2,2048]{2,1,0:T(2,128)(2,1)} %reshape.22) | copy-start | bytes 4718596
  473.9 258.4 %all-reduce.9.cloned.1.call-start = ((), (), s32[]{:S(2)}) async-start(), calls=%async_computation.5 | async-start | bytes 2064384 | tf_op jit(solution)/shard_map/psum | solution.py:45
  676.6 2.0 copy-start
  697.7 124.4 %all-reduce.11.cloned.1.call-start = ((), (), s32[]{:S(2)}) async-start(), calls=%async_computation.6 | async-start | bytes 1179648 | tf_op jit(solution)/shard_map/psum | solution.py:47
  748.0 110.2 %all-reduce.13.cloned.1.call-start = ((), (), s32[]{:S(2)}) async-start(), calls=%async_computation.7 | async-start | bytes 589824 | tf_op jit(solution)/shard_map/psum | solution.py:49
Sparse Core Ops, SparseCore 0:
  10.2 91.8 all-gather.2
  133.1 51.1 reduce-scatter.1
  186.7 26.2 all-gather.4
  474.0 153.1 all-reduce.6
  697.8 34.4 all-reduce.8
  748.1 73.8 all-reduce.10
  826.8 31.3 all-reduce.12
where the time goes:
time: 867 us
  waiting for transfers between devices  439 us (51%)
  blocking collectives  210 us (24%)
  matrix products  153 us (18%)
  other arithmetic  45.3 us (5%)
  between operations  14.3 us (2%)
    psum x1, waiting for transfers between devices, on_device(): range_rows = lax.psum(range_part, 'col')  153 us
    psum x1, blocking collectives, on_device(): lax.psum(jnp.dot(joined, basis_out, preferred_element_type=jnp.float32),...  150 us
    all_gather x1, waiting for transfers between devices, on_device(): full_acts = lax.all_gather(acts, 'col', axis=0, tiled=True)  94.1 us
    psum x1, waiting for transfers between devices, on_device(): core = lax.psum(core_part.astype(jnp.bfloat16), 'col')  74 us
    reduce_scatter x1, waiting for transfers between devices, on_device(): lax.psum_scatter(jnp.einsum('tqi,ij->tqj', rows, basis_in, preferred_elem...  51.3 us
    psum x1, blocking collectives, on_device(): reduced = lax.psum(reduced_part, 'row').astype(jnp.bfloat16)  39.8 us
    psum x1, waiting for transfers between devices, on_device(): mapped = lax.psum(mapped_part.astype(jnp.bfloat16), 'row')  34.3 us
    psum x1, waiting for transfers between devices, on_device(): lax.psum(projection_part.astype(jnp.bfloat16), 'row').astype(jnp.float32)  31.5 us
  transfers between devices with their start and end apart: 7, of which 6 were waited for; matrix products, arithmetic and copies ran while one was open for 3% of the time, Pallas kernels for 0%

commit v1 on v0

--- a/solution.py
+++ b/solution.py
@@ -34,7 +34,11 @@
     reduced_part = jnp.einsum("qjp,sp->qsj", scaled, sketch_rot, preferred_element_type=jnp.float32)
     reduced = lax.psum(reduced_part, "row").astype(jnp.bfloat16)
     range_part = jnp.einsum("qsj,ij->qsi", reduced, basis_in, preferred_element_type=jnp.float32)
-    range_rows = lax.psum(range_part, "col")
+    range_rows = range_part
+    for hop in (1, 2, 4):
+        range_rows = range_rows + lax.ppermute(
+            range_rows, "col", [(dev, dev ^ hop) for dev in range(8)]
+        )
     gram_piece = jnp.einsum("qsi,qri->qsr", range_rows, range_rows, precision=lax.Precision.HIGHEST)
     gram = lax.psum(gram_piece, "row")
     factor = jnp.linalg.cholesky(gram)

time: 867 us -> 1080 us (1.25)
  waiting for transfers between devices: 439 us -> 647 us
    ppermute x0 -> x3, waiting for transfers between devices: none -> 361 us  [on_device(): lax.ppermute(range_rows, 'col', [(dev, dev ^ hop) for dev in range(8)])]
    psum x1 -> x0, waiting for transfers between devices: 153 us -> none  [on_device(): range_rows = lax.psum(range_part, 'col')]
  transfers between devices with their start and end apart: 7 -> 9, of which waited for: 6 -> 8; matrix products, arithmetic and copies ran while one was open for 3% -> 2% of each run, Pallas kernels for 0% -> 0%
where the time goes in v1:
time: 1080 us
  waiting for transfers between devices  647 us (60%)
  blocking collectives  210 us (19%)
  matrix products  149 us (14%)
  other arithmetic  49.1 us (5%)
  between operations  14.3 us (1%)
    ppermute x3, waiting for transfers between devices, on_device(): lax.ppermute(range_rows, 'col', [(dev, dev ^ hop) for dev in range(8)])  361 us
    psum x1, blocking collectives, on_device(): lax.psum(jnp.dot(joined, basis_out, preferred_element_type=jnp.float32),...  150 us
    all_gather x1, waiting for transfers between devices, on_device(): full_acts = lax.all_gather(acts, 'col', axis=0, tiled=True)  94.1 us
    psum x1, waiting for transfers between devices, on_device(): core = lax.psum(core_part.astype(jnp.bfloat16), 'col')  74 us
    reduce_scatter x1, waiting for transfers between devices, on_device(): lax.psum_scatter(jnp.einsum('tqi,ij->tqj', rows, basis_in, preferred_elem...  51.3 us
    psum x1, blocking collectives, on_device(): reduced = lax.psum(reduced_part, 'row').astype(jnp.bfloat16)  39.9 us
    psum x1, waiting for transfers between devices, on_device(): mapped = lax.psum(mapped_part.astype(jnp.bfloat16), 'row')  34.7 us
    psum x1, waiting for transfers between devices, on_device(): lax.psum(projection_part.astype(jnp.bfloat16), 'row').astype(jnp.float32)  31.6 us
  transfers between devices with their start and end apart: 9, of which 8 were waited for; matrix products, arithmetic and copies ran while one was open for 2% of the time, Pallas kernels for 0%

profile of v1, /device:TPU:0, one launch (start us, length us, event | category | flops | bytes accessed | tf_op | source)
XLA Modules:
  0.0 1078.4 jit_solution(6995597473885565088)
XLA Ops:
  7.9 94.1 %all-gather.3.cloned.1.call-done = bf16[192,2,7168]{2,1,0:T(2,128)(2,1)} async-done(((bf16[24,2,7168]{2,1,0:T(2,128)(2,1)}), bf16[192,2,7168]{2,1,0:T(2,128)(2,1)}) %all-gather.3.cloned.1.call-update) | async-done | bytes 5505040 | tf_op jit(solution)/shard_map/all_gather | solution.py:8
  102.0 30.9 %fusion.4 = f32[192,2,3584]{2,0,1:T(8,128)} fusion(bf16[7168,3584]{1,0:T(8,128)(2,1)} %param.8, bf16[192,2,7168]{2,1,0:T(2,128)(2,1)} %all-gather.3.cloned.1.call-done), kind=kOutput, calls=%fused_computation.5 | convolution fusion | flops 19730006016 | bytes 62390272 | tf_op jit(solution)/shard_map/tqi,ij->tqj/dot_general | solution.py:11
  133.0 51.3 %reduce-scatter.2.cloned.1.call-done = f32[48,2,3584]{2,0,1:T(8,128)} async-done(((f32[192,2,3584]{2,0,1:T(8,128)}), f32[48,2,3584]{2,0,1:T(8,128)}) %reduce-scatter.2.cloned.1.call-update) | async-done | bytes 1376272 | tf_op jit(solution)/shard_map/reduce_scatter | solution.py:10
  186.7 8.0 all_gather.9
  195.0 6.2 fusion.18
  201.2 150.4 %all-reduce.11 = bf16[456,2048]{1,0:T(8,128)(2,1)S(1)} all-reduce(f32[456,2048]{1,0:T(8,128)} %fusion.18), channel_id=1, replica_groups=mesh['row'=4,'col'=8] {'col'}, use_global_device_ids=true, to_apply=%region_0.0 | all-reduce | flops 933888 | bytes 5603328 | tf_op jit(solution)/shard_map/psum | solution.py:21
  354.1 16.6 %convert_element_type.32 = f32[3584,2048]{1,0:T(8,128)} convert(bf16[3584,2048]{1,0:T(8,128)(2,1)} %param.10) | non-fusion elementwise | flops 7340032 | bytes 44040192 | tf_op jit(solution)/shard_map/convert_element_type | solution.py:33
  370.8 22.4 %divide_convert_fusion = bf16[2,3584,2048]{2,1,0:T(8,128)(2,1)} fusion(f32[3584,2048]{1,0:T(8,128)} %convert_element_type.32, bf16[192,2,3584]{2,0,1:T(8,128)(2,1)} %all-gather.5.cloned.1.call-done, bf16[192,2,2048]{2,1,0:T(2,128)(2,1)S(1)} %copy-done.3), kind=kOutput, calls=%fused_computation | convolution fusion | flops 5666504704 | bytes 63045632 | tf_op jit(solution)/shard_map/tqj,tqp->qjp/dot_general | solution.py:27
  393.2 14.3 %convolution_bitcast_fusion = f32[2,72,3584]{2,1,0:T(8,128)S(1)} fusion(bf16[2,3584,2048]{2,1,0:T(8,128)(2,1)} %divide_convert_fusion, bf16[456,2048]{1,0:T(8,128)(2,1)} %copy-done.2), kind=kOutput, calls=%fused_computation.8 | convolution fusion | flops 2113929216 | bytes 31719424 | tf_op jit(solution)/shard_map/qjp,sp->qsj/dot_general | solution.py:34
  407.5 39.9 %all-reduce.12 = bf16[2,72,3584]{2,1,0:T(8,128)(2,1)S(1)} all-reduce(f32[2,72,3584]{2,1,0:T(8,128)S(1)} %convolution_bitcast_fusion), channel_id=1, replica_groups=mesh['row'=4,'col'=8] {'row'}, use_global_device_ids=true, to_apply=%region_2.0 | all-reduce | flops 516096 | bytes 3096576 | tf_op jit(solution)/shard_map/psum | solution.py:35
  447.5 26.5 %fusion.2 = f32[2,72,7168]{2,1,0:T(8,128)} fusion(bf16[7168,3584]{1,0:T(8,128)(2,1)} %param.8, bf16[2,72,3584]{2,1,0:T(8,128)(2,1)S(1)} %all-reduce.12), kind=kOutput, calls=%fused_computation.3 | convolution fusion | flops 7398752256 | bytes 56541184 | tf_op jit(solution)/shard_map/qsj,ij->qsi/dot_general | solution.py:36
  474.0 92.0 %collective-permute-done = f32[2,72,7168]{2,1,0:T(8,128)S(1)} collective-permute-done((f32[2,72,7168]{2,1,0:T(8,128)}, f32[2,72,7168]{2,1,0:T(8,128)S(1)}, u32[]{:S(2)}, u32[]{:S(2)}) %collective-permute-start) | collective-permute-done | bytes 4128800 | tf_op jit(solution)/shard_map/ppermute | solution.py:39
  569.1 90.7 %collective-permute-done.1 = f32[2,72,7168]{2,1,0:T(8,128)S(1)} collective-permute-done((f32[2,72,7168]{2,1,0:T(8,128)S(1)}, f32[2,72,7168]{2,1,0:T(8,128)S(1)}, u32[]{:S(2)}, u32[]{:S(2)}) %collective-permute-start.1) | collective-permute-done | bytes 4128800 | tf_op jit(solution)/shard_map/ppermute | solution.py:39
  661.8 178.0 %collective-permute-done.2 = f32[2,72,7168]{2,1,0:T(8,128)S(1)} collective-permute-done((f32[2,72,7168]{2,1,0:T(8,128)S(1)}, f32[2,72,7168]{2,1,0:T(8,128)S(1)}, u32[]{:S(2)}, u32[]{:S(2)}) %collective-permute-start.2) | collective-permute-done | bytes 4128800 | tf_op jit(solution)/shard_map/ppermute | solution.py:39
  846.3 11.6 %psum.44 = f32[2,72,72]{1,2,0:T(8,128)S(1)} all-reduce(f32[2,72,72]{1,2,0:T(8,128)S(1)} %fusion.26), channel_id=1, replica_groups=mesh['row'=4,'col'=8] {'row'}, use_global_device_ids=true, to_apply=%region_3.0 | all-reduce | flops 10368 | bytes 82944 | tf_op jit(solution)/shard_map/psum | solution.py:43
  858.0 13.2 %custom-call.7 = f32[2,72,72]{2,1,0:T(8,128)S(1)} custom-call(f32[2,72,72]{2,1,0:T(8,128)S(1)} %fusion.24), custom_call_target="Cholesky" | custom-call | tf_op jit(solution)/shard_map/jit(cholesky)/cholesky | solution.py:44
  871.5 11.1 %custom-call.8 = f32[2,1,72,72]{2,3,1,0:T(8,128)S(1)} custom-call(f32[2,1,72,72]{3,2,1,0:T(8,128)S(1)} %select_bitcast_fusion), custom_call_target="InvertDiagBlocksLowerTriangular" | custom-call | tf_op jit(solution)/shard_map/triangular_solve | solution.py:45
  882.6 5.3 fusion.22
  889.9 19.0 %fusion.7 = bf16[2,72,3584]{2,1,0:T(8,128)(2,1)} fusion(bf16[7168,3584]{1,0:T(8,128)(2,1)} %param.8, f32[2,72,7168]{2,1,0:T(8,128)S(1)} %fusion.22), kind=kOutput, calls=%fused_computation.9 | convolution fusion | flops 7400300544 | bytes 56541184 | tf_op jit(solution)/shard_map/qsi,ij->qsj/dot_general | solution.py:46
  909.0 34.7 %all-reduce.6.cloned.1.call-done = bf16[2,72,3584]{2,1,0:T(8,128)(2,1)} async-done(((bf16[2,72,3584]{2,1,0:T(8,128)(2,1)}), bf16[2,72,3584]{2,1,0:T(8,128)(2,1)}) %all-reduce.6.cloned.1.call-update) | async-done | bytes 1032208 | tf_op jit(solution)/shard_map/psum | solution.py:49
  943.8 15.7 %convolution_convert_fusion = bf16[2,72,2048]{2,1,0:T(8,128)(2,1)} fusion(bf16[2,72,3584]{2,1,0:T(8,128)(2,1)} %all-reduce.6.cloned.1.call-done, bf16[2,3584,2048]{2,1,0:T(8,128)(2,1)} %divide_convert_fusion), kind=kOutput, calls=%fused_computation.12 | convolution fusion | flops 2114224128 | bytes 30982144 | tf_op jit(solution)/shard_map/qsj,qjp->qsp/dot_general | solution.py:50
  959.6 74.0 %all-reduce.8.cloned.1.call-done = bf16[2,72,2048]{2,1,0:T(8,128)(2,1)} async-done(((bf16[2,72,2048]{2,1,0:T(8,128)(2,1)}), bf16[2,72,2048]{2,1,0:T(8,128)(2,1)}) %all-reduce.8.cloned.1.call-update) | async-done | bytes 589840 | tf_op jit(solution)/shard_map/psum | solution.py:51
  1033.5 4.6 fusion.14
  1038.2 31.6 %all-reduce.10.cloned.1.call-done = bf16[2,72,1024]{2,1,0:T(8,128)(2,1)} async-done(((bf16[2,72,1024]{2,1,0:T(8,128)(2,1)}), bf16[2,72,1024]{2,1,0:T(8,128)(2,1)}) %all-reduce.10.cloned.1.call-update) | async-done | bytes 294928 | tf_op jit(solution)/shard_map/psum | solution.py:53
  (44 shorter events, 21.9 us)
Async XLA Ops:
  7.2 94.9 %all-gather.3.cloned.1.call-start = ((), (), s32[]{:S(2)}) async-start(), calls=%async_computation.1 | async-start | bytes 6193152 | tf_op jit(solution)/shard_map/all_gather | solution.py:8
  7.9 176.4 %reduce-scatter.2.cloned.1.call-start = ((), (), s32[]{:S(2)}) async-start(), calls=%async_computation.2 | async-start | bytes 6881280 | tf_op jit(solution)/shard_map/reduce_scatter | solution.py:10
  133.0 53.7 %copy-start.4 = (bf16[48,2,1024]{2,1,0:T(2,128)(2,1)S(1)}, bf16[48,2,1024]{2,1,0:T(2,128)(2,1)}, u32[]{:S(2)}) copy-start(bf16[48,2,1024]{2,1,0:T(2,128)(2,1)} %param.7) | copy-start | bytes 589828
  133.0 62.0 %copy-start.5 = (bf16[72,1024]{1,0:T(8,128)(2,1)S(1)}, bf16[72,1024]{1,0:T(8,128)(2,1)}, u32[]{:S(2)}) copy-start(bf16[72,1024]{1,0:T(8,128)(2,1)} %param.11) | copy-start | bytes 442372
  133.0 237.8 %all-gather.5.cloned.1.call-start = ((), (), s32[]{:S(2)}) async-start(), calls=%async_computation.3 | async-start | bytes 3440640 | tf_op jit(solution)/shard_map/all_gather | solution.py:29
  186.6 757.2 %all-reduce.6.cloned.1.call-start = ((), (), s32[]{:S(2)}) async-start(), calls=%async_computation.4 | async-start | bytes 2064384 | tf_op jit(solution)/shard_map/psum | solution.py:49
  351.6 19.2 %copy-start.2 = (bf16[456,2048]{1,0:T(8,128)(2,1)}, bf16[456,2048]{1,0:T(8,128)(2,1)S(1)}, u32[]{:S(2)}) copy-start(bf16[456,2048]{1,0:T(8,128)(2,1)S(1)} %all-reduce.11) | copy-start | bytes 5603332
  354.1 16.7 %copy-start.3 = (bf16[192,2,2048]{2,1,0:T(2,128)(2,1)S(1)}, bf16[192,2,2048]{2,1,0:T(2,128)(2,1)}, u32[]{:S(2)}) copy-start(bf16[192,2,2048]{2,1,0:T(2,128)(2,1)} %reshape.22) | copy-start | bytes 4718596
  474.0 92.0 %collective-permute-start = (f32[2,72,7168]{2,1,0:T(8,128)}, f32[2,72,7168]{2,1,0:T(8,128)S(1)}, u32[]{:S(2)}, u32[]{:S(2)}) collective-permute-start(f32[2,72,7168]{2,1,0:T(8,128)} %fusion.2), channel_id=1, source_target_pairs={{0,1},{1,0},{2,3},{3,2},{4,5},{5,4},{6,7},{7,6},{8,9},{9,8},{10,11... | collective-permute-start | bytes 12386312 | tf_op jit(solution)/shard_map/ppermute | solution.py:39
  568.7 91.0 %collective-permute-start.1 = (f32[2,72,7168]{2,1,0:T(8,128)S(1)}, f32[2,72,7168]{2,1,0:T(8,128)S(1)}, u32[]{:S(2)}, u32[]{:S(2)}) collective-permute-start(f32[2,72,7168]{2,1,0:T(8,128)S(1)} %add.34), channel_id=1, source_target_pairs={{0,2},{1,3},{2,0},{3,1},{4,6},{5,7},{6,4},{7,5},{8,10},{9,11},{10,... | collective-permute-start | bytes 12386312 | tf_op jit(solution)/shard_map/ppermute | solution.py:39
  660.3 179.5 %collective-permute-start.2 = (f32[2,72,7168]{2,1,0:T(8,128)S(1)}, f32[2,72,7168]{2,1,0:T(8,128)S(1)}, u32[]{:S(2)}, u32[]{:S(2)}) collective-permute-start(f32[2,72,7168]{2,1,0:T(8,128)S(1)} %add.35), channel_id=1, source_target_pairs={{0,4},{1,5},{2,6},{3,7},{4,0},{5,1},{6,2},{7,3},{8,12},{9,13},{10,... | collective-permute-start | bytes 12386312 | tf_op jit(solution)/shard_map/ppermute | solution.py:39
  840.3 2.0 copy-start
  888.0 2.0 copy-start.1
  909.0 124.6 %all-reduce.8.cloned.1.call-start = ((), (), s32[]{:S(2)}) async-start(), calls=%async_computation.5 | async-start | bytes 1179648 | tf_op jit(solution)/shard_map/psum | solution.py:51
  959.5 110.3 %all-reduce.10.cloned.1.call-start = ((), (), s32[]{:S(2)}) async-start(), calls=%async_computation.6 | async-start | bytes 589824 | tf_op jit(solution)/shard_map/psum | solution.py:53
Sparse Core Ops, SparseCore 0:
  10.2 91.8 all-gather.2
  133.1 51.1 reduce-scatter.1
  186.7 26.2 all-gather.4
  909.1 34.6 all-reduce.5
  959.6 73.8 all-reduce.7
  1038.3 31.3 all-reduce.9
